TPU v7x, 512 devices: a whole 4x4x16 slice. The times are simulated.
512 devices in a mesh: row: 16 (over x_hi, y, core), col: 32 (over z, x_lo).
Axes of the slice: x: 4 (x_hi: 2, x_lo: 2; x = x_hi * 2 + x_lo), y: 4, z: 16, core: 2. Of those that a mesh axis runs over, the one named last changes fastest.
Arguments:
- orbitals: bfloat16 [16384, 2048], P(('row', 'col')), may hold values from -0.125 to 0.125
- coulomb: bfloat16 [16384, 16384], P('row', 'col'), may hold values from -6 to 6
- applied: bfloat16 [16384, 256], P(('row', 'col')), may hold values from -6 to 6
Outputs:
- projectors: float32 [16384, 256], P(('row', 'col'))
All inputs are finite; a program needn't handle non-finite values.
Results may differ from a plain program's by a relative error of at most 0.0029.
Values may be sent and summed in bfloat16 or wider, within the bound.
No kernel may reach another device: no remote copies, remote signals or barrier semaphores. Data moves between devices by JAX's collectives and lax.ppermute only.
A program may use at most 64 MiB of HBM per device.

v0:
```python
import jax
import jax.numpy as jnp
from jax import lax
from jax.sharding import PartitionSpec as P

NMU = 16384


def per_device(orbitals, coulomb, applied):
    point_block = lax.all_gather(orbitals, "col", axis=0, tiled=True)
    paired_orbitals, paired_applied = (
        lax.all_gather(orbitals, "row", axis=0, tiled=True),
        lax.all_gather(applied, "row", axis=0, tiled=True),
    )
    density = jnp.einsum(
        "ik,jk->ij", point_block, paired_orbitals, preferred_element_type=jnp.float32
    )
    kernel = (coulomb.astype(jnp.float32) * density).astype(jnp.bfloat16)
    images = lax.psum_scatter(
        jnp.dot(kernel, paired_applied, preferred_element_type=jnp.float32),
        "col",
        scatter_dimension=0,
        tiled=True,
    )
    local_gram = jnp.einsum("ia,ib->ab", images, images, precision=lax.Precision.HIGHEST)
    gram_sum = lax.psum(local_gram, ("row", "col"))
    gram_matrix = jnp.eye(gram_sum.shape[0], dtype=jnp.float32) + gram_sum / NMU
    factor = jnp.linalg.cholesky(gram_matrix)
    projectors = lax.linalg.triangular_solve(
        factor, images, left_side=False, lower=True, transpose_a=True
    )
    return projectors


def solution(mesh):
    return jax.shard_map(
        per_device,
        mesh=mesh,
        in_specs=(P(("row", "col"), None), P("row", "col"), P(("row", "col"), None)),
        out_specs=P(("row", "col"), None),
        check_vma=False,
    )
```

profile of v0, /device:TPU:4, one launch (start us, length us, event | category | flops | bytes accessed | tf_op | source)
XLA Modules:
  0.0 898.7 jit_solution(3592845915459076260)
XLA Ops:
  6.5 0.7 all-gather.5.cloned.1.call-update
  7.3 0.7 all-gather.3.cloned.1.call-update
  8.1 22.8 %all_gather.11 = bf16[512,256]{1,0:T(8,128)(2,1)S(1)} all-gather(bf16[32,256]{1,0:T(8,128)(2,1)} %param.5), channel_id=1, replica_groups=mesh['row'=16,'col'=32] {'row'}, dimensions={0}, use_global_device_ids=true | all-gather | bytes 278528 | tf_op jit(solution)/shard_map/all_gather | solution.py:13
  30.9 44.7 %all-gather.5.cloned.1.call-done = bf16[512,2048]{1,0:T(8,128)(2,1)} async-done(((bf16[32,2048]{1,0:T(8,128)(2,1)}), bf16[512,2048]{1,0:T(8,128)(2,1)}) %all-gather.5.cloned.1.call-update) | async-done | bytes 2097168 | tf_op jit(solution)/shard_map/all_gather | solution.py:12
  75.6 143.3 %all-gather.3.cloned.1.call-done = bf16[1024,2048]{1,0:T(8,128)(2,1)} async-done(((bf16[32,2048]{1,0:T(8,128)(2,1)}), bf16[1024,2048]{1,0:T(8,128)(2,1)}) %all-gather.3.cloned.1.call-update) | async-done | bytes 4194320 | tf_op jit(solution)/shard_map/all_gather | solution.py:10
  218.8 6.8 fusion
  225.7 0.2 all-reduce.3.cloned.1.call-start
  225.9 134.5 %reduce-scatter.2.cloned.1.call-done = f32[32,256]{1,0:T(8,128)} async-done(((f32[1024,256]{1,0:T(8,128)}), f32[32,256]{1,0:T(8,128)}) %reduce-scatter.2.cloned.1.call-update) | async-done | bytes 32784 | tf_op jit(solution)/shard_map/reduce_scatter | solution.py:19
  360.4 1.9 fusion.10
  362.4 466.6 %all-reduce.3.cloned.1.call-done = f32[256,256]{0,1:T(8,128)} async-done(((f32[256,256]{0,1:T(8,128)}), f32[256,256]{0,1:T(8,128)}) %all-reduce.3.cloned.1.call-update) | async-done | bytes 262160 | tf_op jit(solution)/shard_map/psum | solution.py:26
  829.0 1.0 multiply_add_fusion
  830.2 1.0 fusion.1
  831.2 11.7 %cholesky.50 = f32[128,128]{1,0:T(8,128)S(1)} custom-call(f32[128,128]{1,0:T(8,128)S(1)} %cholesky.118), custom_call_target="Cholesky" | custom-call | tf_op jit(solution)/shard_map/jit(cholesky)/cholesky | solution.py:28
  842.9 9.8 %custom-call.14 = f32[1,128,128]{1,2,0:T(8,128)S(1)} custom-call(f32[1,128,128]{2,1,0:T(8,128)S(1)} %get-tuple-element.26), custom_call_target="InvertDiagBlocksLowerTriangular" | custom-call | tf_op jit(solution)/shard_map/jit(cholesky)/cholesky | solution.py:28
  853.0 0.3 convolution_subtract_fusion
  853.3 11.7 %cholesky.105 = f32[128,128]{1,0:T(8,128)S(1)} custom-call(f32[128,128]{1,0:T(8,128)S(1)} %convolution_subtract_fusion), custom_call_target="Cholesky" | custom-call | tf_op jit(solution)/shard_map/jit(cholesky)/cholesky | solution.py:28
  865.0 0.7 compare_reduce_fusion
  867.1 4.2 while.1
  867.3 0.6 fusion.21
  867.9 1.4 bitcast_dynamic-update-slice_fusion.2
  869.3 0.6 fusion.21
  869.9 1.4 bitcast_dynamic-update-slice_fusion.2
  871.3 19.7 %custom-call.15 = f32[2,128,128]{1,2,0:T(8,128)S(1)} custom-call(f32[2,128,128]{2,1,0:T(8,128)S(1)} %get-tuple-element.12), custom_call_target="InvertDiagBlocksLowerTriangular" | custom-call | tf_op jit(solution)/shard_map/triangular_solve | solution.py:29
  891.5 0.6 pad_maximum_fusion
  (22 shorter events, 1.2 us)
Async XLA Ops:
  6.5 69.0 %all-gather.5.cloned.1.call-start = ((), (), s32[]{:S(2)}) async-start(), calls=%async_computation.2 | async-start | bytes 2228224 | tf_op jit(solution)/shard_map/all_gather | solution.py:12
  7.3 211.6 %all-gather.3.cloned.1.call-start = ((), (), s32[]{:S(2)}) async-start(), calls=%async_computation.1 | async-start | bytes 4325376 | tf_op jit(solution)/shard_map/all_gather | solution.py:10
  8.0 352.4 %reduce-scatter.2.cloned.1.call-start = ((), (), s32[]{:S(2)}) async-start(), calls=%async_computation.3 | async-start | bytes 1081344 | tf_op jit(solution)/shard_map/reduce_scatter | solution.py:19
  225.7 603.4 %all-reduce.3.cloned.1.call-start = ((), (), s32[]{:S(2)}) async-start(), calls=%async_computation.4 | async-start | bytes 524288 | tf_op jit(solution)/shard_map/psum | solution.py:26
  830.0 60.9 %copy-start = (f32[32,256]{1,0:T(8,128)S(1)}, f32[32,256]{1,0:T(8,128)}, u32[]{:S(2)}) copy-start(f32[32,256]{1,0:T(8,128)} %reduce-scatter.2.cloned.1.call-done) | copy-start | bytes 98308
Sparse Core Ops, SparseCore 0:
  10.7 64.8 all-gather.4
  77.6 141.1 all-gather.2
  225.8 134.5 reduce-scatter.1
  365.7 463.2 all-reduce.2
where the time goes:
time: 899 us
  waiting for transfers between devices  791 us (88%)
  other arithmetic  56.3 us (6%)
  blocking collectives  22.8 us (3%)
  between operations  14.5 us (2%)
  matrix products  9.77 us (1%)
    psum x1, waiting for transfers between devices, per_device(): gram_sum = lax.psum(local_gram, ('row', 'col'))  467 us
    all_gather x1, waiting for transfers between devices, per_device(): point_block = lax.all_gather(orbitals, 'col', axis=0, tiled=True)  143 us
    reduce_scatter x1, waiting for transfers between devices, per_device(): lax.psum_scatter(jnp.dot(kernel, paired_applied, preferred_element_type=j...  135 us
    all_gather x1, waiting for transfers between devices, per_device(): lax.all_gather(orbitals, 'row', axis=0, tiled=True)  44.7 us
    another operation x6, other arithmetic, per_device(): factor = jnp.linalg.cholesky(gram_matrix)  34 us
    all_gather x1, blocking collectives, per_device(): lax.all_gather(applied, 'row', axis=0, tiled=True)  22.8 us
    another operation x4, other arithmetic, per_device(): lax.linalg.triangular_solve(factor, images, left_side=False, lower=True,...  20.3 us
  transfers between devices with their start and end apart: 4, of which 4 were waited for; matrix products, arithmetic and copies ran while one was open for 0% of the time, Pallas kernels for 0%

commit v1 on v0

--- a/solution.py
+++ b/solution.py
@@ -7,6 +7,12 @@
 
 
 def per_device(orbitals, coulomb, applied):
+
+    def use_slot(mine_x, mesh_name, dev_axis):
+        for k0 in (mesh_name, dev_axis):
+            mine_x = jax.lax.psum(mine_x, k0)
+        return mine_x
+
     point_block = lax.all_gather(orbitals, "col", axis=0, tiled=True)
     paired_orbitals, paired_applied = (
         lax.all_gather(orbitals, "row", axis=0, tiled=True),
@@ -23,7 +29,7 @@
         tiled=True,
     )
     local_gram = jnp.einsum("ia,ib->ab", images, images, precision=lax.Precision.HIGHEST)
-    gram_sum = lax.psum(local_gram, ("row", "col"))
+    gram_sum = use_slot(local_gram, "row", "col")
     gram_matrix = jnp.eye(gram_sum.shape[0], dtype=jnp.float32) + gram_sum / NMU
     factor = jnp.linalg.cholesky(gram_matrix)
     projectors = lax.linalg.triangular_solve(

time: 899 us -> 854 us (0.950)
  the two profiles are of different devices: /device:TPU:4 before, /device:TPU:8 now
where the time goes in v1:
time: 854 us
  waiting for transfers between devices  743 us (87%)
  other arithmetic  56.3 us (7%)
  blocking collectives  25.6 us (3%)
  between operations  14.5 us (2%)
  matrix products  9.77 us (1%)
    psum x2, waiting for transfers between devices, use_slot(): mine_x = jax.lax.psum(mine_x, k0)  421 us
    all_gather x1, waiting for transfers between devices, per_device(): point_block = lax.all_gather(orbitals, 'col', axis=0, tiled=True)  141 us
    reduce_scatter x1, waiting for transfers between devices, per_device(): lax.psum_scatter(jnp.dot(kernel, paired_applied, preferred_element_type=j...  135 us
    all_gather x1, waiting for transfers between devices, per_device(): lax.all_gather(orbitals, 'row', axis=0, tiled=True)  44 us
    another operation x6, other arithmetic, per_device(): factor = jnp.linalg.cholesky(gram_matrix)  34 us
    all_gather x1, blocking collectives, per_device(): lax.all_gather(applied, 'row', axis=0, tiled=True)  25.6 us
    another operation x4, other arithmetic, per_device(): lax.linalg.triangular_solve(factor, images, left_side=False, lower=True,...  20.3 us
  transfers between devices with their start and end apart: 5, of which 5 were waited for; matrix products, arithmetic and copies ran while one was open for 0% of the time, Pallas kernels for 0%

profile of v1, /device:TPU:8, one launch (start us, length us, event | category | flops | bytes accessed | tf_op | source)
XLA Modules:
  0.0 853.9 jit_solution(14866419415546281674)
XLA Ops:
  6.5 0.7 all-gather.5.cloned.1.call-update
  7.3 0.7 all-gather.3.cloned.1.call-update
  8.1 25.6 %all_gather.11 = bf16[512,256]{1,0:T(8,128)(2,1)S(1)} all-gather(bf16[32,256]{1,0:T(8,128)(2,1)} %param.5), channel_id=1, replica_groups=mesh['row'=16,'col'=32] {'row'}, dimensions={0}, use_global_device_ids=true | all-gather | bytes 278528 | tf_op jit(solution)/shard_map/all_gather | solution.py:19
  33.7 44.0 %all-gather.5.cloned.1.call-done = bf16[512,2048]{1,0:T(8,128)(2,1)} async-done(((bf16[32,2048]{1,0:T(8,128)(2,1)}), bf16[512,2048]{1,0:T(8,128)(2,1)}) %all-gather.5.cloned.1.call-update) | async-done | bytes 2097168 | tf_op jit(solution)/shard_map/all_gather | solution.py:18
  77.7 141.3 %all-gather.3.cloned.1.call-done = bf16[1024,2048]{1,0:T(8,128)(2,1)} async-done(((bf16[32,2048]{1,0:T(8,128)(2,1)}), bf16[1024,2048]{1,0:T(8,128)(2,1)}) %all-gather.3.cloned.1.call-update) | async-done | bytes 4194320 | tf_op jit(solution)/shard_map/all_gather | solution.py:16
  218.9 6.8 fusion
  225.8 135.1 %reduce-scatter.2.cloned.1.call-done = f32[32,256]{1,0:T(8,128)} async-done(((f32[1024,256]{1,0:T(8,128)}), f32[32,256]{1,0:T(8,128)}) %reduce-scatter.2.cloned.1.call-update) | async-done | bytes 32784 | tf_op jit(solution)/shard_map/reduce_scatter | solution.py:25
  360.9 1.9 fusion.10
  363.1 148.3 %all-reduce.4.cloned.1.call-done = f32[256,256]{0,1:T(8,128)} async-done(((f32[256,256]{0,1:T(8,128)}), f32[256,256]{0,1:T(8,128)}) %all-reduce.4.cloned.1.call-update) | async-done | bytes 262160 | tf_op jit(solution)/shard_map/psum | solution.py:13
  511.4 272.9 %all-reduce.6.cloned.1.call-done = f32[256,256]{0,1:T(8,128)} async-done(((f32[256,256]{0,1:T(8,128)}), f32[256,256]{0,1:T(8,128)}) %all-reduce.6.cloned.1.call-update) | async-done | bytes 262160 | tf_op jit(solution)/shard_map/psum | solution.py:13
  784.3 1.0 multiply_add_fusion
  785.4 1.0 fusion.1
  786.4 11.7 %cholesky.50 = f32[128,128]{1,0:T(8,128)S(1)} custom-call(f32[128,128]{1,0:T(8,128)S(1)} %cholesky.118), custom_call_target="Cholesky" | custom-call | tf_op jit(solution)/shard_map/jit(cholesky)/cholesky | solution.py:34
  798.2 9.8 %custom-call.14 = f32[1,128,128]{1,2,0:T(8,128)S(1)} custom-call(f32[1,128,128]{2,1,0:T(8,128)S(1)} %get-tuple-element.26), custom_call_target="InvertDiagBlocksLowerTriangular" | custom-call | tf_op jit(solution)/shard_map/jit(cholesky)/cholesky | solution.py:34
  808.2 0.3 convolution_subtract_fusion
  808.5 11.7 %cholesky.105 = f32[128,128]{1,0:T(8,128)S(1)} custom-call(f32[128,128]{1,0:T(8,128)S(1)} %convolution_subtract_fusion), custom_call_target="Cholesky" | custom-call | tf_op jit(solution)/shard_map/jit(cholesky)/cholesky | solution.py:34
  820.2 0.7 compare_reduce_fusion
  822.3 4.2 while.1
  822.5 0.6 fusion.21
  823.1 1.4 bitcast_dynamic-update-slice_fusion.2
  824.5 0.6 fusion.21
  825.1 1.4 bitcast_dynamic-update-slice_fusion.2
  826.5 19.7 %custom-call.15 = f32[2,128,128]{1,2,0:T(8,128)S(1)} custom-call(f32[2,128,128]{2,1,0:T(8,128)S(1)} %get-tuple-element.12), custom_call_target="InvertDiagBlocksLowerTriangular" | custom-call | tf_op jit(solution)/shard_map/triangular_solve | solution.py:35
  846.7 0.6 pad_maximum_fusion
  (25 shorter events, 1.5 us)
Async XLA Ops:
  6.5 71.1 %all-gather.5.cloned.1.call-start = ((), (), s32[]{:S(2)}) async-start(), calls=%async_computation.2 | async-start | bytes 2228224 | tf_op jit(solution)/shard_map/all_gather | solution.py:18
  7.3 211.7 %all-gather.3.cloned.1.call-start = ((), (), s32[]{:S(2)}) async-start(), calls=%async_computation.1 | async-start | bytes 4325376 | tf_op jit(solution)/shard_map/all_gather | solution.py:16
  8.0 352.9 %reduce-scatter.2.cloned.1.call-start = ((), (), s32[]{:S(2)}) async-start(), calls=%async_computation.3 | async-start | bytes 1081344 | tf_op jit(solution)/shard_map/reduce_scatter | solution.py:25
  225.8 285.6 %all-reduce.4.cloned.1.call-start = ((), (), s32[]{:S(2)}) async-start(), calls=%async_computation.4 | async-start | bytes 524288 | tf_op jit(solution)/shard_map/psum | solution.py:13
  362.8 421.4 %all-reduce.6.cloned.1.call-start = ((), (), s32[]{:S(2)}) async-start(), calls=%async_computation.5 | async-start | bytes 524288 | tf_op jit(solution)/shard_map/psum | solution.py:13
  785.2 60.9 %copy-start = (f32[32,256]{1,0:T(8,128)S(1)}, f32[32,256]{1,0:T(8,128)}, u32[]{:S(2)}) copy-start(f32[32,256]{1,0:T(8,128)} %reduce-scatter.2.cloned.1.call-done) | copy-start | bytes 98308
Sparse Core Ops, SparseCore 0:
  10.7 66.9 all-gather.4
  79.7 139.1 all-gather.2
  225.9 134.9 reduce-scatter.1
  363.6 147.6 all-reduce.3
  514.1 270.1 all-reduce.5
